TPU v7x, 256 devices: a whole 4x4x8 slice. The times are simulated.
256 devices in a mesh: cuts: 8 (over x_lo, y), gz: 32 (over z, x_hi, core).
Axes of the slice: x: 4 (x_hi: 2, x_lo: 2; x = x_hi * 2 + x_lo), y: 4, z: 8, core: 2. Of those that a mesh axis runs over, the one named last changes fastest.
Arguments:
- vectors: float32 [8, 32, 64, 128, 128], P('cuts', None, 'gz'), may hold values from -9 to 9
- onsite: float32 [64, 128, 128], P('gz'), may hold values from -8.25 to 8.25
- center: float32 [8], P('cuts'), may hold values from -3 to 3
- inv_half: float32 [8], P('cuts'), may hold values from 0.06 to 0.1
- cheb_coef: float32 [8, 3], P('cuts'), may hold values from 0.5 to 1.5
Outputs:
- basis: float32 [8, 64, 64, 128, 128], P('cuts', None, 'gz')
- projected: float32 [8, 64, 64], P('cuts')
All inputs are finite; a program needn't handle non-finite values.
Results may differ from a plain program's by a relative error of at most 0.00018.
Values sent between devices are 32-bit elements; how exact they have to be, the bound alone decides.
A program may use at most 128 MiB of HBM per device.

v0:
```python
import jax
import jax.numpy as jnp
from jax import lax
from jax.sharding import PartitionSpec as P


def padded_2(array, sides, width):
    for axis, dim in sides:
        size, length = (lax.axis_size(axis), array.shape[dim])
        up = [(i, (i + 1) % size) for i in range(size)]
        down = [(j, i) for i, j in up]
        last = lax.slice_in_dim(array, length - width, length, axis=dim)
        leading = lax.slice_in_dim(array, 0, width, axis=dim)
        before = lax.ppermute(last, axis, up)
        after = lax.ppermute(leading, axis, down)
        array = jnp.concatenate([before, array, after], axis=dim)
    return array


def from_behind(block, axis, distance):
    devices = range(lax.axis_size(axis))
    route = [(i - distance, i) for i in devices if i - distance in devices]
    return lax.ppermute(block, axis, route)


def neighbours_xy(middle):
    padded = jnp.pad(middle, ((0, 0), (0, 0), (1, 1), (1, 1)))
    return (
        padded[:, :, 2:, 1:-1]
        + padded[:, :, :-2, 1:-1]
        + padded[:, :, 1:-1, 2:]
        + padded[:, :, 1:-1, :-2]
    )


def hamiltonian(extended, onsite_part):
    middle = extended[:, 1:-1]
    along_z = extended[:, 2:] + extended[:, :-2]
    return onsite_part[None] * middle - along_z - neighbours_xy(middle)


def product(left, right):
    return jnp.dot(left, right, precision=lax.Precision.HIGHEST, preferred_element_type=jnp.float32)


def body(vectors, onsite, center, inv_half, cheb_coef):
    field = vectors[0]
    count = field.shape[0]
    layers = field.shape[1]
    sites_all = layers * lax.axis_size("gz") * field.shape[2] * field.shape[3]
    identity = jnp.eye(2 * count, dtype=jnp.float32)

    def scaled(extended, onsite_part):
        return inv_half[0] * (hamiltonian(extended, onsite_part) - center[0] * extended[:, 1:-1])

    def filter_step(values):
        return padded_2(values, (("gz", 1),), 1)

    first = scaled(filter_step(field), onsite)
    second = 2.0 * scaled(filter_step(first), onsite) - field
    filtered = cheb_coef[0, 0] * field + cheb_coef[0, 1] * first + cheb_coef[0, 2] * second
    partner = from_behind(filtered, "cuts", -1)
    union = jnp.concatenate([filtered, partner], 0).reshape(2 * count, -1)
    gram = lax.psum(product(union, union.T), "gz") / sites_all + 0.25 * identity
    factor = jnp.linalg.cholesky(gram)
    inverse = jax.scipy.linalg.solve_triangular(factor, identity, lower=True)
    basis = product(inverse, union)
    shaped = basis.reshape(2 * count, layers, field.shape[2], field.shape[3])
    images = hamiltonian(padded_2(shaped, (("gz", 1),), 1), onsite).reshape(2 * count, -1)
    projected = lax.psum(product(basis, images.T), "gz") / sites_all
    return (basis.reshape(1, 2 * count, layers, field.shape[2], field.shape[3]), projected[None])


def solution(mesh):
    in_specs = (
        P("cuts", None, "gz", None, None),
        P("gz", None, None),
        P("cuts"),
        P("cuts"),
        P("cuts", None),
    )
    out_specs = (P("cuts", None, "gz", None, None), P("cuts", None, None))
    return jax.shard_map(body, mesh=mesh, in_specs=in_specs, out_specs=out_specs, check_vma=False)
```

profile of v0, /device:TPU:24, one launch (start us, length us, event | category | flops | bytes accessed | tf_op | source)
XLA Modules:
  0.0 651.8 jit_solution(12368654120373299613)
XLA Ops:
  0.6 4.6 copy.28
  5.2 0.0 copy-start.5
  5.3 0.4 fusion.38
  5.7 7.8 %collective-permute-start = (f32[32,1,128,128]{3,0,2,1:T(8,128)S(1)}, f32[32,1,128,128]{3,0,2,1:T(8,128)S(1)}, u32[]{:S(2)}, u32[]{:S(2)}) collective-permute-start(f32[32,1,128,128]{3,0,2,1:T(8,128)S(1)} %get-tuple-element.6), channel_id=1, source_target_pairs={{1,0},{2,1},{3,2},{4,3},{5,4},{6,5},{7,6},{8,7},{9,8},{10,9},{11,1... | collective-permute-start | bytes 6291464 | tf_op jit(solution)/shard_map/ppermute | solution.py:15
  13.5 0.0 collective-permute-start.1
  14.8 22.3 %collective-permute-done = f32[32,1,128,128]{3,0,2,1:T(8,128)S(1)} collective-permute-done((f32[32,1,128,128]{3,0,2,1:T(8,128)S(1)}, f32[32,1,128,128]{3,0,2,1:T(8,128)S(1)}, u32[]{:S(2)}, u32[]{:S(2)}) %collective-permute-start) | collective-permute-done | bytes 2097184 | tf_op jit(solution)/shard_map/ppermute | solution.py:15
  37.1 5.6 collective-permute-done.1
  42.7 0.0 copy-done.5
  42.7 3.5 fusion.17
  46.2 0.0 copy-start.6
  46.2 0.0 copy-start.2
  46.2 0.4 fusion.37
  46.7 0.1 collective-permute-start.2
  46.8 34.3 %collective-permute-start.3 = (f32[32,1,128,128]{3,0,2,1:T(8,128)S(1)}, f32[32,1,128,128]{3,0,2,1:T(8,128)S(1)}, u32[]{:S(2)}, u32[]{:S(2)}) collective-permute-start(f32[32,1,128,128]{3,0,2,1:T(8,128)S(1)} %get-tuple-element.5), channel_id=1, source_target_pairs={{0,1},{1,2},{2,3},{3,4},{4,5},{5,6},{6,7},{7,8},{8,9},{9,10},{10,1... | collective-permute-start | bytes 6291464 | tf_op jit(solution)/shard_map/ppermute | solution.py:14
  81.1 0.0 copy-done.6
  81.1 0.7 fusion.39
  81.7 2.9 collective-permute-done.2
  84.6 29.4 %collective-permute-done.3 = f32[32,1,128,128]{3,0,2,1:T(8,128)S(1)} collective-permute-done((f32[32,1,128,128]{3,0,2,1:T(8,128)S(1)}, f32[32,1,128,128]{3,0,2,1:T(8,128)S(1)}, u32[]{:S(2)}, u32[]{:S(2)}) %collective-permute-start.3) | collective-permute-done | bytes 2097184 | tf_op jit(solution)/shard_map/ppermute | solution.py:14
  114.0 0.0 copy-start.4
  114.1 1.3 copy-done.4
  115.4 0.0 copy-done.2
  115.4 9.1 %fusion.27 = f32[32,2,128,128]{3,0,2,1:T(8,128)S(1)} fusion(f32[32,2,128,128]{3,0,2,1:T(8,128)S(1)} %fusion.17, f32[32,1,128,128]{3,0,2,1:T(8,128)} %copy-done.4, f32[32,1,128,128]{3,0,2,1:T(8,128)S(1)} %collective-permute-done.2, f32[]{:T(128)} %bitcast.5, f32[]{:T(128)} %bitcast.44, f32[2,128,128]{2,1,0:T(8,128)S(1)} %copy-done.5, f32[]{:T(128)} %bitcast.46, ...), kind=kLoop, calls=%fused_computation.42 | loop fusion | flops 19922944 | bytes 16908308 | tf_op jit(solution)/shard_map/add | solution.py:61
  124.5 0.0 copy-start.1
  124.5 2.9 collective-permute-start.4
  127.5 74.5 %collective-permute-done.4 = f32[32,2,128,128]{3,0,2,1:T(8,128)S(1)} collective-permute-done((f32[32,2,128,128]{3,0,2,1:T(8,128)S(1)}, f32[32,2,128,128]{3,0,2,1:T(8,128)S(1)}, u32[]{:S(2)}, u32[]{:S(2)}) %collective-permute-start.4) | collective-permute-done | bytes 4194336 | tf_op jit(solution)/shard_map/ppermute | solution.py:23
  202.0 0.0 copy-done.1
  202.0 0.0 copy-start.3
  202.0 2.0 copy-done.3
  204.0 6.6 %convolution_bitcast_fusion = f32[64,64]{1,0:T(8,128)S(1)} fusion(f32[32,2,128,128]{3,0,2,1:T(8,128)S(1)} %collective-permute-done.4, f32[32,2,128,128]{3,0,2,1:T(8,128)S(1)} %fusion.27), kind=kOutput, calls=%fused_computation.52 | convolution fusion | flops 1612709888 | bytes 8404992 | tf_op jit(solution)/shard_map/dot_general | solution.py:43
  210.6 149.8 %psum.14 = f32[64,64]{1,0:T(8,128)S(1)} all-reduce(f32[64,64]{1,0:T(8,128)S(1)} %convolution_bitcast_fusion), channel_id=1, replica_groups=mesh['cuts'=8,'gz'=32] {'gz'}, use_global_device_ids=true, to_apply=%region_0.1 | all-reduce | flops 4096 | bytes 32768 | tf_op jit(solution)/shard_map/psum | solution.py:64
  360.5 4.5 pad_maximum_fusion.2
  365.0 8.3 %copy.11 = f32[64,2,128,128]{3,2,1,0:T(8,128)} copy(f32[64,2,128,128]{3,0,2,1:T(8,128)S(1)} %pad_maximum_fusion.2) | data formatting | bytes 16777216 | tf_op jit(solution)/shard_map/concatenate | solution.py:63
  373.3 0.1 copy.10
  373.4 5.8 cholesky.17
  379.3 0.6 compare_reduce_fusion
  379.9 0.7 fusion.32
  380.6 4.9 custom-call.7
  385.5 0.2 fusion.33
  385.7 16.2 %fusion.7 = f32[64,32768]{1,0:T(8,128)S(1)} fusion(f32[64,64]{1,0:T(8,128)S(1)} %fusion.33, f32[8,8,256,128]{3,2,1,0:T(8,128)} %bitcast.54), kind=kOutput, calls=%fused_computation.19 | convolution fusion | flops 1610612736 | bytes 16793600 | tf_op jit(solution)/shard_map/dot_general | solution.py:43
  401.9 1.5 copy.14
  403.4 0.0 copy-start
  403.4 4.2 fusion.36
  407.6 0.0 collective-permute-start.5
  407.6 0.5 collective-permute-start.6
  408.1 45.9 %collective-permute-done.5 = f32[64,1,128,128]{3,2,1,0:T(8,128)} collective-permute-done((f32[64,1,128,128]{3,2,1,0:T(8,128)}, f32[64,1,128,128]{3,2,1,0:T(8,128)}, u32[]{:S(2)}, u32[]{:S(2)}) %collective-permute-start.5) | collective-permute-done | bytes 4194336 | tf_op jit(solution)/shard_map/ppermute | solution.py:15
  454.0 5.6 collective-permute-done.6
  459.6 0.0 copy-done
  459.6 10.0 %fusion.3 = f32[64,2,128,128]{3,2,1,0:T(8,128)} fusion(f32[64,2,128,128]{3,2,1,0:T(8,128)S(1)} %bitcast.48, f32[64,1,128,128]{3,2,1,0:T(8,128)} %collective-permute-done.6, f32[64,1,128,128]{3,2,1,0:T(8,128)} %collective-permute-done.5, f32[2,128,128]{2,1,0:T(8,128)S(1)} %copy-done.5), kind=kLoop, calls=%fused_computation.15 | loop fusion | flops 18874368 | bytes 25296896 | tf_op jit(solution)/shard_map/sub | solution.py:39
  469.5 15.6 %fusion.4 = f32[64,64]{1,0:T(8,128)S(1)} fusion(f32[64,32768]{1,0:T(8,128)S(1)} %fusion.7, f32[8,8,256,128]{3,2,1,0:T(8,128)} %bitcast.53), kind=kOutput, calls=%fused_computation.16 | convolution fusion | flops 1610612736 | bytes 16793600 | tf_op jit(solution)/shard_map/dot_general | solution.py:43
  485.2 165.7 %psum.15 = f32[64,64]{1,0:T(8,128)S(1)} all-reduce(f32[64,64]{1,0:T(8,128)S(1)} %fusion.4), channel_id=1, replica_groups=mesh['cuts'=8,'gz'=32] {'gz'}, use_global_device_ids=true, to_apply=%region_3.4 | all-reduce | flops 4096 | bytes 32768 | tf_op jit(solution)/shard_map/psum | solution.py:70
  650.9 0.6 multiply_bitcast_fusion
  (3 shorter events, 0.1 us)
Async XLA Ops:
  5.2 37.5 %copy-start.5 = (f32[2,128,128]{2,1,0:T(8,128)S(1)}, f32[2,128,128]{2,1,0:T(8,128)}, u32[]{:S(2)}) copy-start(f32[2,128,128]{2,1,0:T(8,128)} %param.6) | copy-start | bytes 393220
  5.7 31.4 %collective-permute-start = (f32[32,1,128,128]{3,0,2,1:T(8,128)S(1)}, f32[32,1,128,128]{3,0,2,1:T(8,128)S(1)}, u32[]{:S(2)}, u32[]{:S(2)}) collective-permute-start(f32[32,1,128,128]{3,0,2,1:T(8,128)S(1)} %get-tuple-element.6), channel_id=1, source_target_pairs={{1,0},{2,1},{3,2},{4,3},{5,4},{6,5},{7,6},{8,7},{9,8},{10,9},{11,1... | collective-permute-start | bytes 6291464 | tf_op jit(solution)/shard_map/ppermute | solution.py:15
  13.5 29.2 %collective-permute-start.1 = (f32[32,1,128,128]{3,0,2,1:T(8,128)S(1)}, f32[32,1,128,128]{3,0,2,1:T(8,128)S(1)}, u32[]{:S(2)}, u32[]{:S(2)}) collective-permute-start(f32[32,1,128,128]{3,0,2,1:T(8,128)S(1)} %get-tuple-element.7), channel_id=1, source_target_pairs={{0,1},{1,2},{2,3},{3,4},{4,5},{5,6},{6,7},{7,8},{8,9},{9,10},{10,1... | collective-permute-start | bytes 6291464 | tf_op jit(solution)/shard_map/ppermute | solution.py:14
  46.2 34.9 %copy-start.6 = (f32[1,3]{1,0:T(1,128)S(1)}, f32[1,3]{1,0:T(1,128)}, u32[]{:S(2)}) copy-start(f32[1,3]{1,0:T(1,128)} %param.9) | copy-start | bytes 40
  46.2 69.2 %copy-start.2 = (f32[1,32,2,128,128]{4,3,2,1,0:T(8,128)S(1)}, f32[1,32,2,128,128]{4,3,2,1,0:T(8,128)}, u32[]{:S(2)}) copy-start(f32[1,32,2,128,128]{4,3,2,1,0:T(8,128)} %param.5) | copy-start | bytes 12582916
  46.7 38.0 %collective-permute-start.2 = (f32[32,1,128,128]{3,0,2,1:T(8,128)S(1)}, f32[32,1,128,128]{3,0,2,1:T(8,128)S(1)}, u32[]{:S(2)}, u32[]{:S(2)}) collective-permute-start(f32[32,1,128,128]{3,0,2,1:T(8,128)S(1)} %get-tuple-element.4), channel_id=1, source_target_pairs={{1,0},{2,1},{3,2},{4,3},{5,4},{6,5},{7,6},{8,7},{9,8},{10,9},{11,1... | collective-permute-start | bytes 6291464 | tf_op jit(solution)/shard_map/ppermute | solution.py:15
  46.8 67.3 %collective-permute-start.3 = (f32[32,1,128,128]{3,0,2,1:T(8,128)S(1)}, f32[32,1,128,128]{3,0,2,1:T(8,128)S(1)}, u32[]{:S(2)}, u32[]{:S(2)}) collective-permute-start(f32[32,1,128,128]{3,0,2,1:T(8,128)S(1)} %get-tuple-element.5), channel_id=1, source_target_pairs={{0,1},{1,2},{2,3},{3,4},{4,5},{5,6},{6,7},{7,8},{8,9},{9,10},{10,1... | collective-permute-start | bytes 6291464 | tf_op jit(solution)/shard_map/ppermute | solution.py:14
  114.0 1.3 copy-start.4
  124.5 77.5 %copy-start.1 = (f32[32,2,128,128]{3,0,2,1:T(8,128)}, f32[32,2,128,128]{3,0,2,1:T(8,128)S(1)}, u32[]{:S(2)}) copy-start(f32[32,2,128,128]{3,0,2,1:T(8,128)S(1)} %fusion.27) | copy-start | bytes 12582916
  124.5 77.5 %collective-permute-start.4 = (f32[32,2,128,128]{3,0,2,1:T(8,128)S(1)}, f32[32,2,128,128]{3,0,2,1:T(8,128)S(1)}, u32[]{:S(2)}, u32[]{:S(2)}) collective-permute-start(f32[32,2,128,128]{3,0,2,1:T(8,128)S(1)} %fusion.27), channel_id=1, source_target_pairs={{32,0},{64,32},{96,64},{128,96},{160,128},{192,160},{224,192},{33,... | collective-permute-start | bytes 12582920 | tf_op jit(solution)/shard_map/ppermute | solution.py:23
  202.0 2.0 copy-start.3
  403.4 56.1 %copy-start = (f32[8,8,256,128]{3,2,1,0:T(8,128)}, f32[8,8,256,128]{3,2,1,0:T(8,128)S(1)}, u32[]{:S(2)}) copy-start(f32[8,8,256,128]{3,2,1,0:T(8,128)S(1)} %copy.14) | copy-start | bytes 25165828
  407.6 46.4 %collective-permute-start.5 = (f32[64,1,128,128]{3,2,1,0:T(8,128)}, f32[64,1,128,128]{3,2,1,0:T(8,128)}, u32[]{:S(2)}, u32[]{:S(2)}) collective-permute-start(f32[64,1,128,128]{3,2,1,0:T(8,128)} %get-tuple-element.2), channel_id=1, source_target_pairs={{1,0},{2,1},{3,2},{4,3},{5,4},{6,5},{7,6},{8,7},{9,8},{10,9},{11,1... | collective-permute-start | bytes 12582920 | tf_op jit(solution)/shard_map/ppermute | solution.py:15
  407.6 52.0 %collective-permute-start.6 = (f32[64,1,128,128]{3,2,1,0:T(8,128)}, f32[64,1,128,128]{3,2,1,0:T(8,128)}, u32[]{:S(2)}, u32[]{:S(2)}) collective-permute-start(f32[64,1,128,128]{3,2,1,0:T(8,128)} %get-tuple-element.3), channel_id=1, source_target_pairs={{0,1},{1,2},{2,3},{3,4},{4,5},{5,6},{6,7},{7,8},{8,9},{9,10},{10,1... | collective-permute-start | bytes 12582920 | tf_op jit(solution)/shard_map/ppermute | solution.py:14
where the time goes:
time: 659 us; the launch traced here: 652 us
  blocking collectives  316 us (48%)
  waiting for transfers between devices  186 us (28%)
  starting transfers between devices  45.7 us (7%)
  other arithmetic  39.8 us (6%)
  matrix products  38.7 us (6%)
  local copies, waits for them, and re-layouts  23.5 us (4%)
    psum x1, blocking collectives, body(): projected = lax.psum(product(basis, images.T), 'gz') / sites_all  166 us
    psum x1, blocking collectives, body(): gram = lax.psum(product(union, union.T), 'gz') / sites_all + 0.25 * identity  150 us
    ppermute x1, waiting for transfers between devices, from_behind(): return lax.ppermute(block, axis, route)  74.5 us
    ppermute x3, waiting for transfers between devices, padded_2(): after = lax.ppermute(leading, axis, down)  71.1 us
    ppermute x3, waiting for transfers between devices, padded_2(): before = lax.ppermute(last, axis, up)  40.6 us
    dot_general x3, matrix products, product(): jnp.dot(left, right, precision=lax.Precision.HIGHEST, preferred_element_t...  38.5 us
    ppermute x3, starting transfers between devices, padded_2(): before = lax.ppermute(last, axis, up)  34.8 us
  transfers between devices with their start and end apart: 7, of which 7 were waited for; matrix products, arithmetic and copies ran while one was open for 0% of the time, Pallas kernels for 0%

commit v1 on v0

--- a/solution.py
+++ b/solution.py
@@ -67,7 +67,7 @@
     basis = product(inverse, union)
     shaped = basis.reshape(2 * count, layers, field.shape[2], field.shape[3])
     images = hamiltonian(padded_2(shaped, (("gz", 1),), 1), onsite).reshape(2 * count, -1)
-    projected = lax.psum(product(basis, images.T), "gz") / sites_all
+    projected = jnp.sum(lax.all_gather(product(basis, images.T), "gz"), axis=0) / sites_all
     return (basis.reshape(1, 2 * count, layers, field.shape[2], field.shape[3]), projected[None])
 
 

time: 659 us -> 574 us (0.87)
  blocking collectives: 316 us -> 230 us
    psum x1 -> x0, blocking collectives: 166 us -> none  [body(): projected = lax.psum(product(basis, images.T), 'gz') / sites_all]
    all_gather x0 -> x1, blocking collectives: none -> 80 us  [body(): lax.all_gather(product(basis, images.T), 'gz')]
where the time goes in v1:
time: 574 us; the launch traced here: 566 us
  blocking collectives  230 us (40%)
  waiting for transfers between devices  186 us (32%)
  starting transfers between devices  45.7 us (8%)
  other arithmetic  39.9 us (7%)
  matrix products  38.7 us (7%)
  local copies, waits for them, and re-layouts  23.5 us (4%)
    psum x1, blocking collectives, body(): gram = lax.psum(product(union, union.T), 'gz') / sites_all + 0.25 * identity  150 us
    all_gather x1, blocking collectives, body(): lax.all_gather(product(basis, images.T), 'gz')  80 us
    ppermute x1, waiting for transfers between devices, from_behind(): return lax.ppermute(block, axis, route)  74.5 us
    ppermute x3, waiting for transfers between devices, padded_2(): after = lax.ppermute(leading, axis, down)  71.1 us
    ppermute x3, waiting for transfers between devices, padded_2(): before = lax.ppermute(last, axis, up)  40.6 us
    dot_general x3, matrix products, product(): jnp.dot(left, right, precision=lax.Precision.HIGHEST, preferred_element_t...  38.5 us
    ppermute x3, starting transfers between devices, padded_2(): before = lax.ppermute(last, axis, up)  34.8 us
  transfers between devices with their start and end apart: 7, of which 7 were waited for; matrix products, arithmetic and copies ran while one was open for 0% of the time, Pallas kernels for 0%

profile of v1, /device:TPU:24, one launch (start us, length us, event | category | flops | bytes accessed | tf_op | source)
XLA Modules:
  0.0 566.1 jit_solution(8033019109574350952)
XLA Ops:
  0.6 4.6 copy.28
  5.2 0.0 copy-start.5
  5.3 0.4 fusion.38
  5.7 7.8 %collective-permute-start = (f32[32,1,128,128]{3,0,2,1:T(8,128)S(1)}, f32[32,1,128,128]{3,0,2,1:T(8,128)S(1)}, u32[]{:S(2)}, u32[]{:S(2)}) collective-permute-start(f32[32,1,128,128]{3,0,2,1:T(8,128)S(1)} %get-tuple-element.6), channel_id=1, source_target_pairs={{1,0},{2,1},{3,2},{4,3},{5,4},{6,5},{7,6},{8,7},{9,8},{10,9},{11,1... | collective-permute-start | bytes 6291464 | tf_op jit(solution)/shard_map/ppermute | solution.py:15
  13.5 0.0 collective-permute-start.1
  14.8 22.3 %collective-permute-done = f32[32,1,128,128]{3,0,2,1:T(8,128)S(1)} collective-permute-done((f32[32,1,128,128]{3,0,2,1:T(8,128)S(1)}, f32[32,1,128,128]{3,0,2,1:T(8,128)S(1)}, u32[]{:S(2)}, u32[]{:S(2)}) %collective-permute-start) | collective-permute-done | bytes 2097184 | tf_op jit(solution)/shard_map/ppermute | solution.py:15
  37.1 5.6 collective-permute-done.1
  42.7 0.0 copy-done.5
  42.7 3.5 fusion.17
  46.2 0.0 copy-start.6
  46.2 0.0 copy-start.2
  46.2 0.4 fusion.37
  46.7 0.1 collective-permute-start.2
  46.8 34.3 %collective-permute-start.3 = (f32[32,1,128,128]{3,0,2,1:T(8,128)S(1)}, f32[32,1,128,128]{3,0,2,1:T(8,128)S(1)}, u32[]{:S(2)}, u32[]{:S(2)}) collective-permute-start(f32[32,1,128,128]{3,0,2,1:T(8,128)S(1)} %get-tuple-element.5), channel_id=1, source_target_pairs={{0,1},{1,2},{2,3},{3,4},{4,5},{5,6},{6,7},{7,8},{8,9},{9,10},{10,1... | collective-permute-start | bytes 6291464 | tf_op jit(solution)/shard_map/ppermute | solution.py:14
  81.1 0.0 copy-done.6
  81.1 0.7 fusion.39
  81.7 2.9 collective-permute-done.2
  84.6 29.4 %collective-permute-done.3 = f32[32,1,128,128]{3,0,2,1:T(8,128)S(1)} collective-permute-done((f32[32,1,128,128]{3,0,2,1:T(8,128)S(1)}, f32[32,1,128,128]{3,0,2,1:T(8,128)S(1)}, u32[]{:S(2)}, u32[]{:S(2)}) %collective-permute-start.3) | collective-permute-done | bytes 2097184 | tf_op jit(solution)/shard_map/ppermute | solution.py:14
  114.0 0.0 copy-start.4
  114.1 1.3 copy-done.4
  115.4 0.0 copy-done.2
  115.4 9.1 %fusion.27 = f32[32,2,128,128]{3,0,2,1:T(8,128)S(1)} fusion(f32[32,2,128,128]{3,0,2,1:T(8,128)S(1)} %fusion.17, f32[32,1,128,128]{3,0,2,1:T(8,128)} %copy-done.4, f32[32,1,128,128]{3,0,2,1:T(8,128)S(1)} %collective-permute-done.2, f32[]{:T(128)} %bitcast.5, f32[]{:T(128)} %bitcast.45, f32[2,128,128]{2,1,0:T(8,128)S(1)} %copy-done.5, f32[]{:T(128)} %bitcast.47, ...), kind=kLoop, calls=%fused_computation.42 | loop fusion | flops 19922944 | bytes 16908308 | tf_op jit(solution)/shard_map/add | solution.py:61
  124.5 0.0 copy-start.1
  124.5 2.9 collective-permute-start.4
  127.5 74.5 %collective-permute-done.4 = f32[32,2,128,128]{3,0,2,1:T(8,128)S(1)} collective-permute-done((f32[32,2,128,128]{3,0,2,1:T(8,128)S(1)}, f32[32,2,128,128]{3,0,2,1:T(8,128)S(1)}, u32[]{:S(2)}, u32[]{:S(2)}) %collective-permute-start.4) | collective-permute-done | bytes 4194336 | tf_op jit(solution)/shard_map/ppermute | solution.py:23
  202.0 0.0 copy-done.1
  202.0 0.0 copy-start.3
  202.0 2.0 copy-done.3
  204.0 6.6 %convolution_bitcast_fusion = f32[64,64]{1,0:T(8,128)S(1)} fusion(f32[32,2,128,128]{3,0,2,1:T(8,128)S(1)} %collective-permute-done.4, f32[32,2,128,128]{3,0,2,1:T(8,128)S(1)} %fusion.27), kind=kOutput, calls=%fused_computation.52 | convolution fusion | flops 1612709888 | bytes 8404992 | tf_op jit(solution)/shard_map/dot_general | solution.py:43
  210.6 149.8 %psum.7 = f32[64,64]{1,0:T(8,128)S(1)} all-reduce(f32[64,64]{1,0:T(8,128)S(1)} %convolution_bitcast_fusion), channel_id=1, replica_groups=mesh['cuts'=8,'gz'=32] {'gz'}, use_global_device_ids=true, to_apply=%region_0.1 | all-reduce | flops 4096 | bytes 32768 | tf_op jit(solution)/shard_map/psum | solution.py:64
  360.5 4.5 pad_maximum_fusion.2
  365.0 8.3 %copy.11 = f32[64,2,128,128]{3,2,1,0:T(8,128)} copy(f32[64,2,128,128]{3,0,2,1:T(8,128)S(1)} %pad_maximum_fusion.2) | data formatting | bytes 16777216 | tf_op jit(solution)/shard_map/concatenate | solution.py:63
  373.3 0.1 copy.10
  373.4 5.8 %cholesky.17 = f32[64,64]{1,0:T(8,128)S(1)} custom-call(f32[64,64]{1,0:T(8,128)S(1)} %fusion.35), custom_call_target="Cholesky" | custom-call | tf_op jit(solution)/shard_map/jit(cholesky)/cholesky | solution.py:65
  379.3 0.6 compare_reduce_fusion
  379.9 0.7 fusion.32
  380.6 4.9 custom-call.7
  385.5 0.2 fusion.33
  385.7 16.2 %fusion.7 = f32[64,32768]{1,0:T(8,128)S(1)} fusion(f32[64,64]{1,0:T(8,128)S(1)} %fusion.33, f32[8,8,256,128]{3,2,1,0:T(8,128)} %bitcast.55), kind=kOutput, calls=%fused_computation.19 | convolution fusion | flops 1610612736 | bytes 16793600 | tf_op jit(solution)/shard_map/dot_general | solution.py:43
  401.9 1.5 copy.14
  403.4 0.0 copy-start
  403.4 4.2 fusion.36
  407.6 0.0 collective-permute-start.5
  407.6 0.5 collective-permute-start.6
  408.1 45.9 %collective-permute-done.5 = f32[64,1,128,128]{3,2,1,0:T(8,128)} collective-permute-done((f32[64,1,128,128]{3,2,1,0:T(8,128)}, f32[64,1,128,128]{3,2,1,0:T(8,128)}, u32[]{:S(2)}, u32[]{:S(2)}) %collective-permute-start.5) | collective-permute-done | bytes 4194336 | tf_op jit(solution)/shard_map/ppermute | solution.py:15
  454.0 5.6 collective-permute-done.6
  459.6 0.0 copy-done
  459.6 10.0 %fusion.3 = f32[64,2,128,128]{3,2,1,0:T(8,128)} fusion(f32[64,2,128,128]{3,2,1,0:T(8,128)S(1)} %bitcast.49, f32[64,1,128,128]{3,2,1,0:T(8,128)} %collective-permute-done.6, f32[64,1,128,128]{3,2,1,0:T(8,128)} %collective-permute-done.5, f32[2,128,128]{2,1,0:T(8,128)S(1)} %copy-done.5), kind=kLoop, calls=%fused_computation.15 | loop fusion | flops 18874368 | bytes 25296896 | tf_op jit(solution)/shard_map/sub | solution.py:39
  469.5 15.6 %fusion.4 = f32[64,64]{1,0:T(8,128)S(1)} fusion(f32[64,32768]{1,0:T(8,128)S(1)} %fusion.7, f32[8,8,256,128]{3,2,1,0:T(8,128)} %bitcast.54), kind=kOutput, calls=%fused_computation.16 | convolution fusion | flops 1610612736 | bytes 16793600 | tf_op jit(solution)/shard_map/dot_general | solution.py:43
  485.2 80.0 %all-gather = f32[2048,64]{1,0:T(8,128)S(1)} all-gather(f32[64,64]{1,0:T(8,128)S(1)} %fusion.4), channel_id=2, replica_groups=mesh['cuts'=8,'gz'=32] {'gz'}, dimensions={0}, use_global_device_ids=true | all-gather | bytes 540672 | tf_op jit(solution)/shard_map/all_gather | solution.py:70
  565.2 0.1 reduce_sum.9
  565.3 0.6 multiply_bitcast_fusion
  (3 shorter events, 0.1 us)
Async XLA Ops:
  5.2 37.5 %copy-start.5 = (f32[2,128,128]{2,1,0:T(8,128)S(1)}, f32[2,128,128]{2,1,0:T(8,128)}, u32[]{:S(2)}) copy-start(f32[2,128,128]{2,1,0:T(8,128)} %param.6) | copy-start | bytes 393220
  5.7 31.4 %collective-permute-start = (f32[32,1,128,128]{3,0,2,1:T(8,128)S(1)}, f32[32,1,128,128]{3,0,2,1:T(8,128)S(1)}, u32[]{:S(2)}, u32[]{:S(2)}) collective-permute-start(f32[32,1,128,128]{3,0,2,1:T(8,128)S(1)} %get-tuple-element.6), channel_id=1, source_target_pairs={{1,0},{2,1},{3,2},{4,3},{5,4},{6,5},{7,6},{8,7},{9,8},{10,9},{11,1... | collective-permute-start | bytes 6291464 | tf_op jit(solution)/shard_map/ppermute | solution.py:15
  13.5 29.2 %collective-permute-start.1 = (f32[32,1,128,128]{3,0,2,1:T(8,128)S(1)}, f32[32,1,128,128]{3,0,2,1:T(8,128)S(1)}, u32[]{:S(2)}, u32[]{:S(2)}) collective-permute-start(f32[32,1,128,128]{3,0,2,1:T(8,128)S(1)} %get-tuple-element.7), channel_id=1, source_target_pairs={{0,1},{1,2},{2,3},{3,4},{4,5},{5,6},{6,7},{7,8},{8,9},{9,10},{10,1... | collective-permute-start | bytes 6291464 | tf_op jit(solution)/shard_map/ppermute | solution.py:14
  46.2 34.9 %copy-start.6 = (f32[1,3]{1,0:T(1,128)S(1)}, f32[1,3]{1,0:T(1,128)}, u32[]{:S(2)}) copy-start(f32[1,3]{1,0:T(1,128)} %param.9) | copy-start | bytes 40
  46.2 69.2 %copy-start.2 = (f32[1,32,2,128,128]{4,3,2,1,0:T(8,128)S(1)}, f32[1,32,2,128,128]{4,3,2,1,0:T(8,128)}, u32[]{:S(2)}) copy-start(f32[1,32,2,128,128]{4,3,2,1,0:T(8,128)} %param.5) | copy-start | bytes 12582916
  46.7 38.0 %collective-permute-start.2 = (f32[32,1,128,128]{3,0,2,1:T(8,128)S(1)}, f32[32,1,128,128]{3,0,2,1:T(8,128)S(1)}, u32[]{:S(2)}, u32[]{:S(2)}) collective-permute-start(f32[32,1,128,128]{3,0,2,1:T(8,128)S(1)} %get-tuple-element.4), channel_id=1, source_target_pairs={{1,0},{2,1},{3,2},{4,3},{5,4},{6,5},{7,6},{8,7},{9,8},{10,9},{11,1... | collective-permute-start | bytes 6291464 | tf_op jit(solution)/shard_map/ppermute | solution.py:15
  46.8 67.3 %collective-permute-start.3 = (f32[32,1,128,128]{3,0,2,1:T(8,128)S(1)}, f32[32,1,128,128]{3,0,2,1:T(8,128)S(1)}, u32[]{:S(2)}, u32[]{:S(2)}) collective-permute-start(f32[32,1,128,128]{3,0,2,1:T(8,128)S(1)} %get-tuple-element.5), channel_id=1, source_target_pairs={{0,1},{1,2},{2,3},{3,4},{4,5},{5,6},{6,7},{7,8},{8,9},{9,10},{10,1... | collective-permute-start | bytes 6291464 | tf_op jit(solution)/shard_map/ppermute | solution.py:14
  114.0 1.3 copy-start.4
  124.5 77.5 %copy-start.1 = (f32[32,2,128,128]{3,0,2,1:T(8,128)}, f32[32,2,128,128]{3,0,2,1:T(8,128)S(1)}, u32[]{:S(2)}) copy-start(f32[32,2,128,128]{3,0,2,1:T(8,128)S(1)} %fusion.27) | copy-start | bytes 12582916
  124.5 77.5 %collective-permute-start.4 = (f32[32,2,128,128]{3,0,2,1:T(8,128)S(1)}, f32[32,2,128,128]{3,0,2,1:T(8,128)S(1)}, u32[]{:S(2)}, u32[]{:S(2)}) collective-permute-start(f32[32,2,128,128]{3,0,2,1:T(8,128)S(1)} %fusion.27), channel_id=1, source_target_pairs={{32,0},{64,32},{96,64},{128,96},{160,128},{192,160},{224,192},{33,... | collective-permute-start | bytes 12582920 | tf_op jit(solution)/shard_map/ppermute | solution.py:23
  202.0 2.0 copy-start.3
  403.4 56.1 %copy-start = (f32[8,8,256,128]{3,2,1,0:T(8,128)}, f32[8,8,256,128]{3,2,1,0:T(8,128)S(1)}, u32[]{:S(2)}) copy-start(f32[8,8,256,128]{3,2,1,0:T(8,128)S(1)} %copy.14) | copy-start | bytes 25165828
  407.6 46.4 %collective-permute-start.5 = (f32[64,1,128,128]{3,2,1,0:T(8,128)}, f32[64,1,128,128]{3,2,1,0:T(8,128)}, u32[]{:S(2)}, u32[]{:S(2)}) collective-permute-start(f32[64,1,128,128]{3,2,1,0:T(8,128)} %get-tuple-element.2), channel_id=1, source_target_pairs={{1,0},{2,1},{3,2},{4,3},{5,4},{6,5},{7,6},{8,7},{9,8},{10,9},{11,1... | collective-permute-start | bytes 12582920 | tf_op jit(solution)/shard_map/ppermute | solution.py:15
  407.6 52.0 %collective-permute-start.6 = (f32[64,1,128,128]{3,2,1,0:T(8,128)}, f32[64,1,128,128]{3,2,1,0:T(8,128)}, u32[]{:S(2)}, u32[]{:S(2)}) collective-permute-start(f32[64,1,128,128]{3,2,1,0:T(8,128)} %get-tuple-element.3), channel_id=1, source_target_pairs={{0,1},{1,2},{2,3},{3,4},{4,5},{5,6},{6,7},{7,8},{8,9},{9,10},{10,1... | collective-permute-start | bytes 12582920 | tf_op jit(solution)/shard_map/ppermute | solution.py:14
